TPU v7x, 128 devices: a whole 4x4x4 slice. The times are simulated.
128 devices in a mesh: tile: 64 (over z, y, x), slide: 2 (over core).
Axes of the slice: x: 4, y: 4, z: 4, core: 2. Of those that a mesh axis runs over, the one named last changes fastest.
Arguments:
- features: bfloat16 [256, 32, 32, 256], P(('slide', 'tile')), parts along dimension 0, may hold values from -8 to 8
- neighbours: int32 [256, 8], P(('slide', 'tile')), parts along dimension 0, may hold values from 0 to 128, as said below
- conv_weight: bfloat16 [3, 3, 256, 256], replicated, may hold values from -0.125 to 0.125
- patch_weight: bfloat16 [4096, 768], replicated, may hold values from -1 to 1
- query_weight: bfloat16 [768, 768], replicated, may hold values from -2 to 2
- key_weight: bfloat16 [768, 768], replicated, may hold values from -2 to 2
- value_weight: bfloat16 [768, 768], replicated, may hold values from -0.21875 to 0.21875
- output_weight: bfloat16 [768, 768], replicated, may hold values from -0.21875 to 0.21875
- cotangent: bfloat16 [16384, 768], P(('slide', 'tile')), parts along dimension 0, may hold values from -6 to 6
Outputs:
- mixed: bfloat16 [16384, 768], P(('slide', 'tile')), parts along dimension 0
- output_grad: float32 [1536, 768], P('slide'), parts along dimension 0
There are 2 independent parts, one for each index of `slide`. A program takes and returns all parts, laid end to end along the dimension named above; an argument that names none is the same for every part. Nothing has to cross between parts.
Inputs may be any that keep to these rules, and one draw needn't show every extreme that they name: Tiles are tissue cells of a grid 16 cells wide; the tile numbers are given to the tissue cells in a drawn order, so neighbours may have any numbers; each entry is the index of the tissue tile at that grid offset, or 128.
All inputs are finite; a program needn't handle non-finite values.
Results may differ from a plain program's by a relative error of at most 0.02.
Values may be sent and summed in bfloat16 or wider, within the bound.
No kernel may reach another device: no remote copies, remote signals or barrier semaphores. Data moves between devices by JAX's collectives and lax.ppermute only.
A program may use at most 192 MiB of HBM per device.

v0:
```python
import jax
import jax.numpy as jnp
from jax import lax
from jax.sharding import PartitionSpec as P

PATCH = 4
HEADS = 12
HD = 64


def tile_faces(maps):
    return jnp.stack([maps[:, 0], maps[:, -1], maps[:, :, 0], maps[:, :, -1]], axis=1)


def pad_tiles(maps, all_faces, links):
    upper = all_faces[links[:, 1], 1]
    lower = all_faces[links[:, 6], 0]
    left_col = all_faces[links[:, 3], 3]
    right_col = all_faces[links[:, 4], 2]
    corner_ul = all_faces[links[:, 0], 1, -1]
    corner_ur = all_faces[links[:, 2], 1, 0]
    corner_dl = all_faces[links[:, 5], 0, -1]
    corner_dr = all_faces[links[:, 7], 0, 0]
    top_row = jnp.concatenate([corner_ul[:, None], upper, corner_ur[:, None]], axis=1)
    bottom_row = jnp.concatenate([corner_dl[:, None], lower, corner_dr[:, None]], axis=1)
    middle = jnp.concatenate([left_col[:, :, None], maps, right_col[:, :, None]], axis=2)
    return jnp.concatenate([top_row[:, None], middle, bottom_row[:, None]], axis=1)


def conv_tiles(padded, kernel):
    count = padded.shape[0]
    side = padded.shape[1] - 2
    chans = padded.shape[3]
    total = jnp.zeros((count * side * side, kernel.shape[3]), jnp.float32)
    for row_off in range(3):
        for col_off in range(3):
            window = padded[:, row_off : row_off + side, col_off : col_off + side, :].reshape(
                -1, chans
            )
            total = total + jnp.dot(
                window, kernel[row_off, col_off], preferred_element_type=jnp.float32
            )
    return jax.nn.gelu(total).astype(jnp.bfloat16).reshape(count, side, side, -1)


def patchify(hidden, patch):
    count, side, _, chans = hidden.shape
    blocks = side // patch
    grid = hidden.reshape(count, blocks, patch, blocks, patch, chans).transpose(0, 1, 3, 2, 4, 5)
    return grid.reshape(count * blocks * blocks, patch * patch * chans)


def local(
    features,
    neighbours,
    conv_weight,
    patch_weight,
    query_weight,
    key_weight,
    value_weight,
    output_weight,
    cotangent,
):
    local_faces = tile_faces(features)
    gathered = lax.all_gather(local_faces, "tile", axis=0, tiled=True)
    all_faces = jnp.concatenate(
        [gathered, jnp.zeros((1,) + gathered.shape[1:], jnp.bfloat16)], axis=0
    )
    padded = pad_tiles(features, all_faces, neighbours)
    hidden = conv_tiles(padded, conv_weight)
    tokens = jnp.dot(
        patchify(hidden, PATCH), patch_weight, preferred_element_type=jnp.float32
    ).astype(jnp.bfloat16)
    rows = tokens.shape[0]
    query = (
        jnp.dot(tokens, query_weight, preferred_element_type=jnp.float32)
        .astype(jnp.bfloat16)
        .reshape(rows, HEADS, HD)
    )
    scale = HD ** (-0.5)
    keys = jnp.dot(tokens, key_weight, preferred_element_type=jnp.float32).astype(jnp.bfloat16)
    values = jnp.dot(tokens, value_weight, preferred_element_type=jnp.float32).astype(jnp.bfloat16)
    top = jnp.full((HEADS, rows), -1e30, jnp.float32)
    key_heads = lax.all_gather(keys, "tile", axis=0, tiled=True).reshape(-1, HEADS, HD)
    value_heads = lax.all_gather(values, "tile", axis=0, tiled=True).reshape(-1, HEADS, HD)
    scores = (
        jnp.einsum("qhd,khd->hqk", query, key_heads, preferred_element_type=jnp.float32) * scale
    )
    new_top = jnp.maximum(top, jnp.max(scores, axis=-1))
    weights = jnp.exp(scores - new_top[..., None])
    total = jnp.sum(weights, axis=-1)
    accum = jnp.einsum(
        "hqk,khd->hqd",
        weights.astype(jnp.bfloat16),
        value_heads,
        preferred_element_type=jnp.float32,
    )
    top, total, accum = (new_top, total, accum)
    attended = (
        (accum / total[..., None]).transpose(1, 0, 2).reshape(rows, HEADS * HD).astype(jnp.bfloat16)
    )
    mixed = (
        tokens.astype(jnp.float32)
        + jnp.dot(attended, output_weight, preferred_element_type=jnp.float32)
    ).astype(jnp.bfloat16)
    grad_term = jnp.dot(attended.T, cotangent, preferred_element_type=jnp.float32)
    output_grad = lax.psum(grad_term, "tile")
    return (mixed, output_grad)


def solution(mesh):
    in_specs = (
        P(("slide", "tile"), None, None, None),
        P(("slide", "tile"), None),
        P(),
        P(),
        P(),
        P(),
        P(),
        P(),
        P(("slide", "tile"), None),
    )
    out_specs = (P(("slide", "tile"), None), P("slide", None))
    return jax.shard_map(local, mesh=mesh, in_specs=in_specs, out_specs=out_specs, check_vma=False)
```

profile of v0, /device:TPU:0, one launch (start us, length us, event | category | flops | bytes accessed | tf_op | source)
XLA Modules:
  0.0 506.7 jit_solution(2070060483644725372)
XLA Ops:
  7.2 1.2 fusion.78
  8.5 0.8 fusion.77
  9.3 0.7 pad_maximum_fusion.3
  10.0 1.3 fusion.68
  11.3 81.0 %all-gather.4.cloned.1.call-done = bf16[128,4,32,256]{3,2,1,0:T(8,128)(2,1)} async-done(((bf16[2,4,32,256]{3,2,1,0:T(8,128)(2,1)}), bf16[128,4,32,256]{3,2,1,0:T(8,128)(2,1)}) %all-gather.4.cloned.1.call-update) | async-done | bytes 8388624 | tf_op jit(solution)/shard_map/all_gather | solution.py:65
  92.3 8.5 %concatenate.53 = bf16[129,4,32,256]{3,2,1,0:T(8,128)(2,1)} pad(bf16[128,4,32,256]{3,2,1,0:T(8,128)(2,1)} %all-gather.4.cloned.1.call-done, bf16[]{:T(256)} %constant.15.clone.1), padding=0_1x0_0x0_0x0_0 | pad | bytes 16842754 | tf_op jit(solution)/shard_map/concatenate | solution.py:66
  100.8 3.9 gather_fusion.1
  104.8 1.5 gather_fusion
  106.3 1.5 gather_fusion.2
  107.8 3.9 gather_fusion.6
  111.7 1.5 gather_fusion.5
  113.2 1.5 gather_fusion.7
  114.7 3.9 gather_fusion.3
  118.7 4.0 gather_fusion.4
  122.7 1.2 pad_maximum_fusion.1
  124.0 1.7 pad_maximum_fusion
  125.7 0.8 fusion.76
  126.5 0.8 fusion.75
  127.2 0.5 copy-done.5
  127.7 0.4 fusion.32
  128.2 0.4 convolution_add_fusion.7
  128.6 0.4 convolution_add_fusion.6
  129.1 0.4 convolution_add_fusion.5
  129.5 0.4 convolution_add_fusion.4
  129.9 0.4 convolution_add_fusion.3
  130.4 0.4 convolution_add_fusion.2
  130.8 0.5 convolution_add_fusion.1
  131.3 0.9 fusion.13
  132.2 0.3 reshape_reshape.3
  132.5 0.4 copy.60
  132.9 0.8 reshape.58
  133.7 3.8 convolution_convert_fusion.3
  137.5 1.0 convolution_convert_fusion.1
  138.6 2.3 convolution_convert_fusion
  140.9 0.2 all-reduce.8.cloned.1.call-start
  141.2 0.3 convolution_convert_fusion.2
  141.5 0.2 copy.52
  141.7 87.6 %all-gather.6.cloned.1.call-done = bf16[8192,768]{1,0:T(8,128)(2,1)} async-done(((bf16[128,768]{1,0:T(8,128)(2,1)}), bf16[8192,768]{1,0:T(8,128)(2,1)}) %all-gather.6.cloned.1.call-update) | async-done | bytes 12582928 | tf_op jit(solution)/shard_map/all_gather | solution.py:84
  229.2 15.8 %copy.53 = bf16[8192,768]{0,1:T(8,128)(2,1)} copy(bf16[8192,768]{1,0:T(8,128)(2,1)} %all-gather.6.cloned.1.call-done) | data formatting | bytes 25165824 | tf_op jit(solution)/shard_map/all_gather | solution.py:84
  245.0 22.0 %multiply_reduce_fusion = (f32[12,128]{1,0:T(8,128)S(1)}, f32[12,128,8192]{2,1,0:T(8,128)}) fusion(bf16[128,12,64]{0,2,1:T(8,128)(2,1)S(1)} %bitcast.106, bf16[8192,12,64]{0,2,1:T(8,128)(2,1)} %bitcast.92), kind=kOutput, calls=%fused_computation.9 | convolution fusion | flops 1635777024 | bytes 63117312 | tf_op jit(solution)/shard_map/qhd,khd->hqk/dot_general | solution.py:87
  267.0 21.7 %fusion = f32[12,128]{1,0:T(8,128)S(1)} fusion(f32[12,128,8192]{2,1,0:T(8,128)} %get-tuple-element.25, f32[12,128]{1,0:T(8,128)S(1)} %broadcast_maximum_fusion), kind=kLoop, calls=%fused_computation.10 | loop fusion | flops 37747200 | bytes 50343936 | tf_op jit(solution)/shard_map/reduce_sum | solution.py:91
  288.8 34.3 %all-gather.8.cloned.1.call-done = bf16[8192,768]{1,0:T(8,128)(2,1)} async-done(((bf16[128,768]{1,0:T(8,128)(2,1)}), bf16[8192,768]{1,0:T(8,128)(2,1)}) %all-gather.8.cloned.1.call-update) | async-done | bytes 12582928 | tf_op jit(solution)/shard_map/all_gather | solution.py:85
  323.1 15.8 %copy.54 = bf16[8192,768]{0,1:T(8,128)(2,1)} copy(bf16[8192,768]{1,0:T(8,128)(2,1)} %all-gather.8.cloned.1.call-done) | data formatting | bytes 25165824 | tf_op jit(solution)/shard_map/all_gather | solution.py:85
  338.9 22.2 %fusion.21 = bf16[128,12,64]{0,2,1:T(8,128)(2,1)S(1)} fusion(bf16[8192,12,64]{0,2,1:T(8,128)(2,1)} %bitcast.93, f32[12,128,8192]{2,1,0:T(8,128)} %get-tuple-element.25, f32[12,128]{1,0:T(8,128)S(1)} %broadcast_maximum_fusion, f32[128,12]{0,1:T(8,128)S(1)} %bitcast.109), kind=kOutput, calls=%fused_computation.42 | convolution fusion | flops 1648558080 | bytes 63123456 | tf_op jit(solution)/shard_map/hqk,khd->hqd/dot_general | solution.py:92
  361.1 1.9 fusion.79
  363.0 1.0 fusion.17
  364.1 132.8 %all-reduce.8.cloned.1.call-done = f32[768,768]{1,0:T(8,128)} async-done(((f32[768,768]{1,0:T(8,128)}), f32[768,768]{1,0:T(8,128)}) %all-reduce.8.cloned.1.call-update) | async-done | bytes 2359312 | tf_op jit(solution)/shard_map/psum | solution.py:107
  496.9 3.2 copy.62
  (30 shorter events, 0.4 us)
Async XLA Ops:
  7.2 130.3 %copy-start = (bf16[768,768]{1,0:T(8,128)(2,1)S(1)}, bf16[768,768]{1,0:T(8,128)(2,1)}, u32[]{:S(2)}) copy-start(bf16[768,768]{1,0:T(8,128)(2,1)} %param.14) | copy-start | bytes 3538948
  7.2 85.1 %all-gather.4.cloned.1.call-start = ((), (), s32[]{:S(2)}) async-start(), calls=%async_computation | async-start | bytes 8519680 | tf_op jit(solution)/shard_map/all_gather | solution.py:65
  10.0 219.3 %all-gather.6.cloned.1.call-start = ((), (), s32[]{:S(2)}) async-start(), calls=%async_computation.1 | async-start | bytes 12779520 | tf_op jit(solution)/shard_map/all_gather | solution.py:84
  11.3 111.4 %copy-start.2 = (bf16[2,32,32,256]{3,2,1,0:T(8,128)(2,1)S(1)}, bf16[2,32,32,256]{3,2,1,0:T(8,128)(2,1)}, u32[]{:S(2)}) copy-start(bf16[2,32,32,256]{3,2,1,0:T(8,128)(2,1)} %param.9) | copy-start | bytes 3145732
  126.5 1.3 copy-start.5
  137.5 3.6 copy-start.3
  138.6 184.5 %all-gather.8.cloned.1.call-start = ((), (), s32[]{:S(2)}) async-start(), calls=%async_computation.2 | async-start | bytes 12779520 | tf_op jit(solution)/shard_map/all_gather | solution.py:85
  140.9 356.0 %all-reduce.8.cloned.1.call-start = ((), (), s32[]{:S(2)}) async-start(), calls=%async_computation.3 | async-start | bytes 4718592 | tf_op jit(solution)/shard_map/psum | solution.py:107
  338.9 22.2 %copy-start.6 = (bf16[128,768]{1,0:T(8,128)(2,1)S(1)}, bf16[128,768]{1,0:T(8,128)(2,1)}, u32[]{:S(2)}) copy-start(bf16[128,768]{1,0:T(8,128)(2,1)} %param.17) | copy-start | bytes 589828
  361.1 1.9 copy-start.4
  363.0 137.1 %copy-start.1 = (bf16[768,768]{1,0:T(8,128)(2,1)S(1)}, bf16[768,768]{1,0:T(8,128)(2,1)}, u32[]{:S(2)}) copy-start(bf16[768,768]{1,0:T(8,128)(2,1)} %param.14) | copy-start | bytes 3538948
Sparse Core Ops, SparseCore 0:
  11.4 80.8 all-gather.3
  138.7 90.4 all-gather.5
  232.5 90.5 all-gather.7
  363.1 133.7 all-reduce.7
where the time goes:
time: 508 us; the launch traced here: 507 us
  waiting for transfers between devices  336 us (66%)
  local copies, waits for them, and re-layouts  70.9 us (14%)
  matrix products  58.9 us (12%)
  other arithmetic  26.6 us (5%)
  between operations  14 us (3%)
    psum x1, waiting for transfers between devices, local(): output_grad = lax.psum(grad_term, 'tile')  133 us
    all_gather x1, waiting for transfers between devices, local(): lax.all_gather(keys, 'tile', axis=0, tiled=True).reshape(-1, HEADS, HD)  87.6 us
    all_gather x1, waiting for transfers between devices, local(): gathered = lax.all_gather(local_faces, 'tile', axis=0, tiled=True)  81 us
    all_gather x1, waiting for transfers between devices, local(): lax.all_gather(values, 'tile', axis=0, tiled=True).reshape(-1, HEADS, HD)  34.3 us
    dot_general x1, matrix products, local(): jnp.einsum('hqk,khd->hqd', weights.astype(jnp.bfloat16), value_heads, pre...  22.2 us
    dot_general x1, matrix products, local(): jnp.einsum('qhd,khd->hqk', query, key_heads, preferred_element_type=jnp.f...  22 us
    reduce_sum x1, other arithmetic, local(): total = jnp.sum(weights, axis=-1)  21.7 us
    all_gather x1, local copies, waits for them, and re-layouts, local(): lax.all_gather(keys, 'tile', axis=0, tiled=True).reshape(-1, HEADS, HD)  15.8 us
  transfers between devices with their start and end apart: 4, of which 4 were waited for; matrix products, arithmetic and copies ran while one was open for 13% of the time, Pallas kernels for 0%

commit v1 on v0

--- a/solution.py
+++ b/solution.py
@@ -81,7 +81,9 @@
     keys = jnp.dot(tokens, key_weight, preferred_element_type=jnp.float32).astype(jnp.bfloat16)
     values = jnp.dot(tokens, value_weight, preferred_element_type=jnp.float32).astype(jnp.bfloat16)
     top = jnp.full((HEADS, rows), -1e30, jnp.float32)
-    key_heads = lax.all_gather(keys, "tile", axis=0, tiled=True).reshape(-1, HEADS, HD)
+    key_heads = jnp.concatenate(
+        lax.all_to_all(jnp.stack([keys] * lax.axis_size("tile")), "tile", 0, 0), axis=0
+    ).reshape(-1, HEADS, HD)
     value_heads = lax.all_gather(values, "tile", axis=0, tiled=True).reshape(-1, HEADS, HD)
     scores = (
         jnp.einsum("qhd,khd->hqk", query, key_heads, preferred_element_type=jnp.float32) * scale

time: 508 us -> 634 us (1.25)
  waiting for transfers between devices: 336 us -> 429 us
  local copies, waits for them, and re-layouts: 70.9 us -> 96.6 us
  starting transfers between devices: 0.35 us -> 9.09 us
    all_to_all x0 -> x1, waiting for transfers between devices: none -> 202 us  [local(): lax.all_to_all(jnp.stack([keys] * lax.axis_size('tile')), 'tile', 0, 0)]
    all_gather x1 -> x0, waiting for transfers between devices: 87.6 us -> none  [local(): lax.all_gather(keys, 'tile', axis=0, tiled=True).reshape(-1, HEADS, HD)]
    all_gather x1, waiting for transfers between devices: 34.3 us -> 0.02 us  [local(): lax.all_gather(values, 'tile', axis=0, tiled=True).reshape(-1, HEADS, HD)]
    another operation x0 -> x2, local copies, waits for them, and re-layouts: none -> 26.8 us  [the longest x1 19.3 us: local(): key_heads = jnp.concatenate(lax.all_to_all(jnp.stack([keys] * lax.axis_si...]
    all_gather x1 -> x0, local copies, waits for them, and re-layouts: 15.8 us -> none  [local(): lax.all_gather(keys, 'tile', axis=0, tiled=True).reshape(-1, HEADS, HD)]
    all_to_all x0 -> x1, local copies, waits for them, and re-layouts: none -> 14.5 us  [local(): lax.all_to_all(jnp.stack([keys] * lax.axis_size('tile')), 'tile', 0, 0)]
    psum x1, waiting for transfers between devices: 133 us -> 146 us  [local(): output_grad = lax.psum(grad_term, 'tile')]
    all_to_all x0 -> x1, starting transfers between devices: none -> 8.96 us  [local(): lax.all_to_all(jnp.stack([keys] * lax.axis_size('tile')), 'tile', 0, 0)]
  transfers between devices with their start and end apart: 4 -> 4, of which waited for: 4 -> 3; matrix products, arithmetic and copies ran while one was open for 13% -> 14% of each run, Pallas kernels for 0% -> 0%
where the time goes in v1:
time: 634 us; the launch traced here: 633 us
  waiting for transfers between devices  429 us (68%)
  local copies, waits for them, and re-layouts  96.6 us (15%)
  matrix products  58 us (9%)
  other arithmetic  25.6 us (4%)
  between operations  14.1 us (2%)
  starting transfers between devices  9.09 us (1%)
    all_to_all x1, waiting for transfers between devices, local(): lax.all_to_all(jnp.stack([keys] * lax.axis_size('tile')), 'tile', 0, 0)  202 us
    psum x1, waiting for transfers between devices, local(): output_grad = lax.psum(grad_term, 'tile')  146 us
    all_gather x1, waiting for transfers between devices, local(): gathered = lax.all_gather(local_faces, 'tile', axis=0, tiled=True)  81 us
    dot_general x1, matrix products, local(): jnp.einsum('hqk,khd->hqd', weights.astype(jnp.bfloat16), value_heads, pre...  22.2 us
    dot_general x1, matrix products, local(): jnp.einsum('qhd,khd->hqk', query, key_heads, preferred_element_type=jnp.f...  21.7 us
    reduce_sum x1, other arithmetic, local(): total = jnp.sum(weights, axis=-1)  20.5 us
    another operation x1, local copies, waits for them, and re-layouts, local(): key_heads = jnp.concatenate(lax.all_to_all(jnp.stack([keys] * lax.axis_si...  19.3 us
    all_gather x1, local copies, waits for them, and re-layouts, local(): lax.all_gather(values, 'tile', axis=0, tiled=True).reshape(-1, HEADS, HD)  15.8 us
  transfers between devices with their start and end apart: 4, of which 3 were waited for; matrix products, arithmetic and copies ran while one was open for 14% of the time, Pallas kernels for 0%

profile of v1, /device:TPU:0, one launch (start us, length us, event | category | flops | bytes accessed | tf_op | source)
XLA Modules:
  0.0 632.6 jit_solution(10034574884031518418)
XLA Ops:
  7.2 1.2 fusion.78
  8.5 0.8 fusion.77
  9.3 0.7 pad_maximum_fusion.3
  10.0 1.3 fusion.68
  11.3 81.0 %all-gather.3.cloned.1.call-done = bf16[128,4,32,256]{3,2,1,0:T(8,128)(2,1)} async-done(((bf16[2,4,32,256]{3,2,1,0:T(8,128)(2,1)}), bf16[128,4,32,256]{3,2,1,0:T(8,128)(2,1)}) %all-gather.3.cloned.1.call-update) | async-done | bytes 8388624 | tf_op jit(solution)/shard_map/all_gather | solution.py:65
  92.3 8.5 %concatenate.53 = bf16[129,4,32,256]{3,2,1,0:T(8,128)(2,1)} pad(bf16[128,4,32,256]{3,2,1,0:T(8,128)(2,1)} %all-gather.3.cloned.1.call-done, bf16[]{:T(256)} %constant.15.clone.1), padding=0_1x0_0x0_0x0_0 | pad | bytes 16842754 | tf_op jit(solution)/shard_map/concatenate | solution.py:66
  100.8 3.9 gather_fusion.1
  104.8 1.5 gather_fusion
  106.3 1.5 gather_fusion.2
  107.8 3.9 gather_fusion.6
  111.7 1.5 gather_fusion.5
  113.2 1.5 gather_fusion.7
  114.7 3.9 gather_fusion.3
  118.7 4.0 gather_fusion.4
  122.7 1.2 pad_maximum_fusion.1
  124.0 1.9 pad_maximum_fusion
  125.9 0.8 fusion.76
  126.7 0.8 fusion.75
  127.4 0.5 copy-done.5
  127.9 0.4 fusion.32
  128.3 0.4 convolution_add_fusion.7
  128.8 0.4 convolution_add_fusion.6
  129.2 0.4 convolution_add_fusion.5
  129.7 0.4 convolution_add_fusion.4
  130.1 0.4 convolution_add_fusion.3
  130.6 0.4 convolution_add_fusion.2
  131.0 0.4 convolution_add_fusion.1
  131.4 0.9 fusion.13
  132.4 0.3 reshape_reshape.6
  132.6 0.4 copy.61
  133.1 0.8 reshape.57
  133.9 3.8 convolution_convert_fusion.3
  137.7 1.0 convolution_convert_fusion
  138.7 1.6 convolution_convert_fusion.1
  140.5 7.5 %stack.5 = bf16[64,128,768]{1,2,0:T(8,128)(2,1)} broadcast(bf16[128,768]{0,1:T(8,128)(2,1)S(1)} %copy.53), dimensions={1,2} | broadcast | bytes 12779520 | tf_op jit(solution)/shard_map/stack | solution.py:85
  148.0 9.0 %all-to-all-start = ((bf16[64,128,768]{1,2,0:T(8,128)(2,1)}), bf16[64,128,768]{1,2,0:T(8,128)(2,1)}, u32[]{:S(2)}, u32[]{:S(2)}) async-start(bf16[64,128,768]{1,2,0:T(8,128)(2,1)} %stack.5), calls=%async_computation | async-start | bytes 25165824 | tf_op jit(solution)/shard_map/all_to_all | solution.py:85
  157.0 0.3 convolution_convert_fusion.2
  157.5 202.2 %all-to-all-done = bf16[64,128,768]{1,2,0:T(8,128)(2,1)} async-done(((bf16[64,128,768]{1,2,0:T(8,128)(2,1)}), bf16[64,128,768]{1,2,0:T(8,128)(2,1)}, u32[]{:S(2)}, u32[]{:S(2)}) %all-to-all-start) | async-done | bytes 12582944 | tf_op jit(solution)/shard_map/all_to_all | solution.py:85
  359.8 14.5 %copy.54 = bf16[64,128,768]{1,0,2:T(8,128)(2,1)} copy(bf16[64,128,768]{1,2,0:T(8,128)(2,1)} %all-to-all-done) | data formatting | bytes 25165824 | tf_op jit(solution)/shard_map/all_to_all | solution.py:85
  374.3 19.3 %reshape_reshape.7 = bf16[8192,12,64]{0,2,1:T(8,128)(2,1)} reshape(bf16[64,128,768]{1,0,2:T(8,128)(2,1)} %copy.54) | data formatting | bytes 25165824 | tf_op jit(solution)/shard_map/reshape;reshape | solution.py:86
  393.6 21.7 %multiply_reduce_fusion = (f32[12,128]{1,0:T(8,128)S(1)}, f32[12,128,8192]{2,1,0:T(8,128)}) fusion(bf16[128,12,64]{0,2,1:T(8,128)(2,1)S(1)} %bitcast.106, bf16[8192,12,64]{0,2,1:T(8,128)(2,1)} %reshape_reshape.7), kind=kOutput, calls=%fused_computation.9 | convolution fusion | flops 1635777024 | bytes 63117312 | tf_op jit(solution)/shard_map/qhd,khd->hqk/dot_general | solution.py:89
  415.3 20.5 %fusion = f32[12,128]{1,0:T(8,128)S(1)} fusion(f32[12,128,8192]{2,1,0:T(8,128)} %get-tuple-element.25, f32[12,128]{1,0:T(8,128)S(1)} %broadcast_maximum_fusion), kind=kLoop, calls=%fused_computation.10 | loop fusion | flops 37747200 | bytes 50343936 | tf_op jit(solution)/shard_map/reduce_sum | solution.py:93
  435.8 15.8 %copy.55 = bf16[8192,768]{0,1:T(8,128)(2,1)} copy(bf16[8192,768]{1,0:T(8,128)(2,1)} %all-gather.5.cloned.1.call-done) | data formatting | bytes 25165824 | tf_op jit(solution)/shard_map/all_gather | solution.py:87
  451.6 22.2 %fusion.21 = bf16[128,12,64]{0,2,1:T(8,128)(2,1)S(1)} fusion(bf16[8192,12,64]{0,2,1:T(8,128)(2,1)} %bitcast.93, f32[12,128,8192]{2,1,0:T(8,128)} %get-tuple-element.25, f32[12,128]{1,0:T(8,128)S(1)} %broadcast_maximum_fusion, f32[128,12]{0,1:T(8,128)S(1)} %bitcast.109), kind=kOutput, calls=%fused_computation.42 | convolution fusion | flops 1648558080 | bytes 63123456 | tf_op jit(solution)/shard_map/hqk,khd->hqd/dot_general | solution.py:94
  473.9 1.9 fusion.79
  475.8 1.0 fusion.17
  476.8 146.1 %all-reduce.8.cloned.1.call-done = f32[768,768]{1,0:T(8,128)} async-done(((f32[768,768]{1,0:T(8,128)}), f32[768,768]{1,0:T(8,128)}) %all-reduce.8.cloned.1.call-update) | async-done | bytes 2359312 | tf_op jit(solution)/shard_map/psum | solution.py:109
  622.9 3.2 copy.63
  (32 shorter events, 0.7 us)
Async XLA Ops:
  7.2 130.5 %copy-start = (bf16[768,768]{1,0:T(8,128)(2,1)S(1)}, bf16[768,768]{1,0:T(8,128)(2,1)}, u32[]{:S(2)}) copy-start(bf16[768,768]{1,0:T(8,128)(2,1)} %param.15) | copy-start | bytes 3538948
  7.2 85.1 %all-gather.3.cloned.1.call-start = ((), (), s32[]{:S(2)}) async-start(), calls=%async_computation.1 | async-start | bytes 8519680 | tf_op jit(solution)/shard_map/all_gather | solution.py:65
  10.0 425.9 %all-gather.5.cloned.1.call-start = ((), (), s32[]{:S(2)}) async-start(), calls=%async_computation.2 | async-start | bytes 12779520 | tf_op jit(solution)/shard_map/all_gather | solution.py:87
  11.3 111.4 %copy-start.2 = (bf16[2,32,32,256]{3,2,1,0:T(8,128)(2,1)S(1)}, bf16[2,32,32,256]{3,2,1,0:T(8,128)(2,1)}, u32[]{:S(2)}) copy-start(bf16[2,32,32,256]{3,2,1,0:T(8,128)(2,1)} %param.9) | copy-start | bytes 3145732
  126.6 1.3 copy-start.5
  148.0 9.0 %copy-start.3 = (bf16[768,768]{1,0:T(8,128)(2,1)S(1)}, bf16[768,768]{1,0:T(8,128)(2,1)}, u32[]{:S(2)}) copy-start(bf16[768,768]{1,0:T(8,128)(2,1)} %param.13) | copy-start | bytes 3538948
  148.0 211.8 %all-to-all-start = ((bf16[64,128,768]{1,2,0:T(8,128)(2,1)}), bf16[64,128,768]{1,2,0:T(8,128)(2,1)}, u32[]{:S(2)}, u32[]{:S(2)}) async-start(bf16[64,128,768]{1,2,0:T(8,128)(2,1)} %stack.5), calls=%async_computation | async-start | bytes 25165824 | tf_op jit(solution)/shard_map/all_to_all | solution.py:85
  157.0 465.9 %all-reduce.8.cloned.1.call-start = ((), (), s32[]{:S(2)}) async-start(), calls=%async_computation.3 | async-start | bytes 4718592 | tf_op jit(solution)/shard_map/psum | solution.py:109
  451.6 22.2 %copy-start.6 = (bf16[128,768]{1,0:T(8,128)(2,1)S(1)}, bf16[128,768]{1,0:T(8,128)(2,1)}, u32[]{:S(2)}) copy-start(bf16[128,768]{1,0:T(8,128)(2,1)} %param.17) | copy-start | bytes 589828
  473.9 1.9 copy-start.4
  475.8 150.3 %copy-start.1 = (bf16[768,768]{1,0:T(8,128)(2,1)S(1)}, bf16[768,768]{1,0:T(8,128)(2,1)}, u32[]{:S(2)}) copy-start(bf16[768,768]{1,0:T(8,128)(2,1)} %param.15) | copy-start | bytes 3538948
Sparse Core Ops, SparseCore 0:
  11.4 80.8 all-gather.2
  138.8 234.0 all-gather.4
  475.9 146.9 all-reduce.7
